TPU v7x, 32 devices: a whole 2x2x4 slice. The times are simulated.
32 devices in a mesh: dp: 4 (over y, core), expert: 8 (over z, x).
Axes of the slice: x: 2, y: 2, z: 4, core: 2. Of those that a mesh axis runs over, the one named last changes fastest.
Arguments:
- tokens: bfloat16 [1024, 7168], P('expert', 'dp'), may hold values from -6 to 6
- routes: int32 [1024, 8], P('expert'), may hold values from 0 to 31, all different within a row; in each aligned block of 128 rows (0 to 127, 128 to 255, ...) at most 64 rows name the same one
- route_weight: float32 [1024, 8], P('expert'), may hold values from 0.1 to 1
- gate_first: bfloat16 [32, 64, 112, 32], P('expert', 'dp'), may hold values from -0.5 to 0.5
- up_first: bfloat16 [32, 64, 112, 32], P('expert', 'dp'), may hold values from -0.5 to 0.5
- gate_second: bfloat16 [32, 32, 64, 64], P('expert', 'dp'), may hold values from -0.75 to 0.75
- up_second: bfloat16 [32, 32, 64, 64], P('expert', 'dp'), may hold values from -0.75 to 0.75
- down_first: bfloat16 [32, 32, 64, 64], P('expert', 'dp'), may hold values from -0.75 to 0.75
- down_second: bfloat16 [32, 64, 32, 112], P('expert', 'dp'), may hold values from -1 to 1
Outputs:
- moe_output: bfloat16 [1024, 7168], P('expert', 'dp')
- expert_load: float32 [32], P('expert')
Inputs may be any that keep to these rules, and one draw needn't show every extreme that they name: `routes`: each row names 8 different experts. Within each device's aligned block of 128 rows no expert is named by more than 64 rows, and in some block an expert is named by exactly 64 rows.
All inputs are finite; a program needn't handle non-finite values.
Results may differ from a plain program's by a relative error of at most 0.0076.
Values may be sent and summed in bfloat16 or wider, within the bound.
A program may use at most 64 MiB of HBM per device.

v0:
```python
import jax
import jax.numpy as jnp
from jax import lax
from jax.sharding import PartitionSpec as P


def shards(
    tokens,
    routes,
    route_weight,
    gate_first,
    up_first,
    gate_second,
    up_second,
    down_first,
    down_second,
):
    tok_rows, width_here = tokens.shape
    top_k = routes.shape[1]
    groups = lax.axis_size("expert")
    dp_count = lax.axis_size("dp")
    per_dev, blocks_here, block_width, rank_size = gate_first.shape
    rank_here = gate_second.shape[1]
    block_count = gate_second.shape[2]
    experts = per_dev * groups
    capacity = 2 * tok_rows * top_k // experts
    flat_routes = routes.reshape(-1)
    pair_count = flat_routes.shape[0]
    one_hot = (flat_routes[:, None] == jnp.arange(experts, dtype=jnp.int32)[None, :]).astype(
        jnp.int32
    )
    earlier = jnp.cumsum(one_hot, axis=0) - one_hot
    position = jnp.sum(earlier * one_hot, axis=1)
    counts = jnp.sum(one_hot, axis=0)
    slot_index = flat_routes * capacity + position
    pair_token = jnp.arange(pair_count, dtype=jnp.int32) // top_k
    slot_token = jnp.full((experts * capacity,), tok_rows, jnp.int32).at[slot_index].set(pair_token)
    outgoing = jnp.take(tokens, slot_token, axis=0, mode="fill", fill_value=0).reshape(
        groups, per_dev, capacity, width_here
    )
    gate_wide = gate_second.reshape(per_dev, rank_here, dp_count, blocks_here, block_count)
    up_wide = up_second.reshape(per_dev, rank_here, dp_count, blocks_here, block_count)
    down_wide = down_second.reshape(per_dev, blocks_here, dp_count, rank_here, block_width)
    received = lax.all_to_all(outgoing, "expert", split_axis=0, concat_axis=0, tiled=True)
    sources = received.shape[0]
    local = received.shape[1]
    slots = received.shape[2]
    split_rows = received.reshape(sources, local, slots, blocks_here, block_width)
    gate_low = jnp.einsum(
        "aesbf,ebfr->rbeas", split_rows, gate_first, preferred_element_type=jnp.float32
    )
    up_low = jnp.einsum(
        "aesbf,ebfr->rbeas", split_rows, up_first, preferred_element_type=jnp.float32
    )
    layout = (dp_count, rank_here, blocks_here, local, sources, slots)
    gate_mixed = lax.all_to_all(
        gate_low.astype(jnp.bfloat16).reshape(layout), "dp", split_axis=0, concat_axis=0, tiled=True
    )
    up_mixed = lax.all_to_all(
        up_low.astype(jnp.bfloat16).reshape(layout), "dp", split_axis=0, concat_axis=0, tiled=True
    )
    gate_high = jnp.einsum(
        "qcjeas,ecqjm->ecmas", gate_mixed, gate_wide, preferred_element_type=jnp.float32
    )
    up_high = jnp.einsum(
        "qcjeas,ecqjm->ecmas", up_mixed, up_wide, preferred_element_type=jnp.float32
    )
    activated = (jax.nn.silu(gate_high) * up_high).astype(jnp.bfloat16)
    down_low = jnp.einsum(
        "ecmas,ecmn->ecnas", activated, down_first, preferred_element_type=jnp.float32
    )
    down_split = down_low.astype(jnp.bfloat16).reshape(
        local, rank_here, dp_count, blocks_here, sources, slots
    )
    down_mixed = lax.all_to_all(down_split, "dp", split_axis=2, concat_axis=2, tiled=True)
    expert_out = jnp.einsum(
        "ecqjas,ejqcf->aesjf", down_mixed, down_wide, preferred_element_type=jnp.float32
    )
    result = expert_out.astype(jnp.bfloat16).reshape(sources, local, slots, width_here)
    totals = lax.psum(counts, "expert")
    own_counts = lax.dynamic_slice_in_dim(
        totals, lax.axis_index("expert") * per_dev, per_dev
    ).astype(jnp.float32)
    returned = lax.all_to_all(result, "expert", split_axis=0, concat_axis=0, tiled=True).reshape(
        experts * capacity, width_here
    )
    picked = jnp.take(returned, slot_index, axis=0).astype(jnp.float32)
    weighted = picked * route_weight.reshape(-1)[:, None]
    moe_output = jnp.sum(weighted.reshape(tok_rows, top_k, width_here), axis=1).astype(jnp.bfloat16)
    expert_load = own_counts * experts / (tok_rows * groups * top_k)
    return (moe_output, expert_load)


def solution(mesh):
    return jax.shard_map(
        shards,
        mesh=mesh,
        in_specs=(
            P("expert", "dp"),
            P("expert", None),
            P("expert", None),
            P("expert", "dp", None, None),
            P("expert", "dp", None, None),
            P("expert", "dp", None, None),
            P("expert", "dp", None, None),
            P("expert", "dp", None, None),
            P("expert", "dp", None, None),
        ),
        out_specs=(P("expert", "dp"), P("expert")),
        check_vma=False,
    )
```

profile of v0, /device:TPU:0, one launch (start us, length us, event | category | flops | bytes accessed | tf_op | source)
XLA Modules:
  0.0 615.8 jit_solution(15726805077561847400)
XLA Ops:
  2.6 9.0 %reduce-window.6 = s32[32,8,128]{2,1,0:T(8,128)S(1)} reduce-window(s32[32,8,128]{2,1,0:T(8,128)S(1)} %fusion.33, s32[]{:T(128)} %constant.59.clone.1), window={size=1x1x128 pad=0_0x0_0x127_0}, to_apply=%region_0.0 | reduce-window | flops 4161536 | bytes 262148 | tf_op jit(solution)/shard_map/reduce-window
  12.2 4.3 scatter_custom_fusion
  16.7 10.7 %gather_fusion = bf16[2048,1792]{1,0:T(8,128)(2,1)} fusion(bf16[128,1792]{1,0:T(8,128)(2,1)S(1)} %copy-done.1, s32[2048]{0:T(1024)S(1)} %fusion.34), kind=kCustom, calls=%fused_computation | custom fusion | bytes 14688256 | tf_op jit(solution)/shard_map/jit(_take)/gather | solution.py:38
  27.3 3.7 broadcast_select_fusion
  31.0 168.0 %all_to_all.25 = bf16[8,4,64,1792]{3,2,1,0:T(8,128)(2,1)} all-to-all(bf16[8,4,64,1792]{3,2,1,0:T(8,128)(2,1)S(1)} %broadcast_select_fusion), channel_id=1, replica_groups=mesh['dp'=4,'expert'=8] {'expert'}, dimensions={0} | all-to-all | bytes 14680064 | tf_op jit(solution)/shard_map/all_to_all | solution.py:44
  199.0 17.4 %reshape.113 = bf16[8,4,64,16,112]{4,3,2,1,0:T(8,128)(2,1)} reshape(bf16[8,4,64,1792]{3,2,1,0:T(8,128)(2,1)} %all_to_all.25) | data formatting | bytes 14680064 | tf_op jit(solution)/shard_map/reshape | solution.py:48
  216.4 11.2 %convert_bitcast_fusion.2 = bf16[4,8,16,4,8,64]{5,1,0,4,3,2:T(8,128)(2,1)S(1)} fusion(bf16[8,4,64,16,112]{4,3,2,1,0:T(8,128)(2,1)} %reshape.113, bf16[4,16,112,32]{2,3,1,0:T(8,128)(2,1)S(1)} %copy-done.2), kind=kOutput, calls=%fused_computation.28 | convolution fusion | flops 235929600 | bytes 9895936 | tf_op jit(solution)/shard_map/aesbf,ebfr->rbeas/dot_general | solution.py:49
  227.6 4.7 copy.139
  232.3 6.0 reshape.158
  238.3 3.9 all-to-all-start.1
  242.2 11.2 %convert_bitcast_fusion.1 = bf16[4,8,16,4,8,64]{5,1,0,4,3,2:T(8,128)(2,1)S(1)} fusion(bf16[8,4,64,16,112]{4,3,2,1,0:T(8,128)(2,1)} %reshape.113, bf16[4,16,112,32]{2,3,1,0:T(8,128)(2,1)S(1)} %copy-done.3), kind=kOutput, calls=%fused_computation.27 | convolution fusion | flops 235929600 | bytes 9895936 | tf_op jit(solution)/shard_map/aesbf,ebfr->rbeas/dot_general | solution.py:52
  256.5 5.9 reshape.160
  262.5 5.3 all-to-all-done.1
  267.8 4.9 all-to-all-start.2
  272.7 4.0 reshape.159
  276.8 6.7 %fusion.13 = f32[4,8,8,64,64,1]{4,3,1,0,2,5:T(8,128)} fusion(bf16[4,8,4,16,64,1]{4,3,2,1,0,5:T(8,128)(2,1)S(1)} %bitcast.113, bf16[4,4,8,8,16,64]{5,4,3,2,1,0:T(8,128)(2,1)} %reshape.159), kind=kOutput, calls=%fused_computation.22 | convolution fusion | flops 134217728 | bytes 6553600 | tf_op jit(solution)/shard_map/qcjeas,ecqjm->ecmas/dot_general | solution.py:62
  283.5 14.9 %all-to-all-done.2 = bf16[4,2,131072]{2,1,0:T(2,128)(2,1)} async-done(((bf16[4,2,131072]{2,1,0:T(2,128)(2,1)}), bf16[4,2,131072]{2,1,0:T(2,128)(2,1)}, u32[]{:S(2)}, u32[]{:S(2)}) %all-to-all-start.2) | async-done | bytes 2097184 | tf_op jit(solution)/shard_map/all_to_all | solution.py:59
  298.4 5.8 reshape.161
  304.2 10.8 %fusion.1 = bf16[4,8,64,8,64]{2,4,0,3,1:T(8,128)(2,1)S(1)} fusion(f32[4,8,8,64,64,1]{4,3,1,0,2,5:T(8,128)} %fusion.13, bf16[4,8,16,4,8,64]{5,1,4,3,2,0:T(8,128)(2,1)} %bitcast.112, bf16[4,8,4,16,64,1]{4,3,2,1,0,5:T(8,128)(2,1)S(1)} %bitcast.119), kind=kOutput, calls=%fused_computation.6 | convolution fusion | flops 140509184 | bytes 8650752 | tf_op jit(solution)/shard_map/qcjeas,ecqjm->ecmas/dot_general | solution.py:65
  318.2 6.6 %copy.67 = bf16[4,8,64,8,64]{4,3,2,1,0:T(8,128)(2,1)} copy(bf16[4,8,64,8,64]{2,4,3,1,0:T(8,128)(2,1)} %convert_bitcast_fusion) | data formatting | bytes 4194304 | tf_op jit(solution)/shard_map/convert_element_type | solution.py:72
  324.9 10.8 %copy.137 = bf16[4,8,4,16,8,64]{5,1,4,3,0,2:T(8,128)(2,1)} copy(bf16[4,8,4,16,8,64]{5,4,3,2,1,0:T(8,128)(2,1)} %bitcast.110) | data formatting | bytes 4194304 | tf_op jit(solution)/shard_map/reshape | solution.py:72
  335.7 4.9 reshape.162
  340.6 28.9 %all_to_all.26 = bf16[4,2,131072]{2,1,0:T(2,128)(2,1)} all-to-all(bf16[4,2,131072]{2,1,0:T(2,128)(2,1)S(1)} %reshape.162), channel_id=1, replica_groups=mesh['dp'=4,'expert'=8] {'dp'}, dimensions={0} | all-to-all | bytes 4194304 | tf_op jit(solution)/shard_map/all_to_all | solution.py:75
  369.5 6.0 reshape.163
  375.5 7.8 %fusion.9 = bf16[4,16,8,64,112,1]{4,3,1,0,2,5:T(8,128)(2,1)} fusion(bf16[4,4,16,8,8,64]{5,4,3,2,1,0:T(8,128)(2,1)} %reshape.163, bf16[4,16,32,112]{3,2,1,0:T(8,128)(2,1)S(1)} %copy-done), kind=kOutput, calls=%fused_computation.18 | convolution fusion | flops 234881024 | bytes 9895936 | tf_op jit(solution)/shard_map/ecqjas,ejqcf->aesjf/dot_general | solution.py:76
  383.3 9.6 %copy.136 = bf16[4,16,8,64,112,1]{4,3,0,2,1,5:T(8,128)(2,1)} copy(bf16[4,16,8,64,112,1]{4,3,1,0,2,5:T(8,128)(2,1)} %fusion.9) | data formatting | bytes 14680064 | tf_op jit(solution)/shard_map/ecqjas,ejqcf->aesjf/dot_general | solution.py:76
  393.0 23.1 %copy.71 = bf16[8,4,64,16,112]{4,3,2,1,0:T(8,128)(2,1)} copy(bf16[8,4,64,16,112]{4,2,1,0,3:T(8,128)(2,1)} %bitcast.106) | data formatting | bytes 14680064 | tf_op jit(solution)/shard_map/convert_element_type | solution.py:79
  416.1 15.2 %reshape.120 = bf16[8,4,64,1792]{3,2,1,0:T(8,128)(2,1)} reshape(bf16[8,4,64,16,112]{4,3,2,1,0:T(8,128)(2,1)} %copy.71) | data formatting | bytes 14680064 | tf_op jit(solution)/shard_map/reshape | solution.py:79
  431.3 5.0 all-to-all-start.4
  436.7 160.5 %psum.7 = s32[32]{0:T(128)S(1)} all-reduce(s32[32]{0:T(128)S(1)} %get-tuple-element.2), channel_id=1, replica_groups=mesh['dp'=4,'expert'=8] {'expert'}, use_global_device_ids=true, to_apply=%region_6.7 | all-reduce | flops 32 | bytes 256 | tf_op jit(solution)/shard_map/psum | solution.py:80
  597.8 12.0 %gather_fusion.1 = bf16[1024,1792]{1,0:T(8,128)(2,1)} fusion(bf16[2048,1792]{1,0:T(8,128)(2,1)} %bitcast.28, s32[1024]{0:T(1024)S(1)} %broadcast_clamp_fusion), kind=kCustom, calls=%fused_computation.1 | custom fusion | bytes 7344128 | tf_op jit(solution)/shard_map/jit(_take)/gather | solution.py:87
  609.8 5.6 multiply_reduce_fusion
  (47 shorter events, 10.0 us)
Async XLA Ops:
  0.6 374.9 %copy-start = (bf16[4,16,32,112]{3,2,1,0:T(8,128)(2,1)S(1)}, bf16[4,16,32,112]{3,2,1,0:T(8,128)(2,1)}, u32[]{:S(2)}) copy-start(bf16[4,16,32,112]{3,2,1,0:T(8,128)(2,1)} %param.17) | copy-start | bytes 1376260
  0.6 16.0 %copy-start.1 = (bf16[128,1792]{1,0:T(8,128)(2,1)S(1)}, bf16[128,1792]{1,0:T(8,128)(2,1)}, u32[]{:S(2)}) copy-start(bf16[128,1792]{1,0:T(8,128)(2,1)} %param.9) | copy-start | bytes 1376260
  199.0 17.4 %copy-start.2 = (bf16[4,16,112,32]{2,3,1,0:T(8,128)(2,1)S(1)}, bf16[4,16,112,32]{2,3,1,0:T(8,128)(2,1)}, u32[]{:S(2)}) copy-start(bf16[4,16,112,32]{2,3,1,0:T(8,128)(2,1)} %param.12) | copy-start | bytes 1376260
  232.3 9.8 %copy-start.3 = (bf16[4,16,112,32]{2,3,1,0:T(8,128)(2,1)S(1)}, bf16[4,16,112,32]{2,3,1,0:T(8,128)(2,1)}, u32[]{:S(2)}) copy-start(bf16[4,16,112,32]{2,3,1,0:T(8,128)(2,1)} %param.13) | copy-start | bytes 1376260
  238.3 29.5 %all-to-all-start.1 = ((bf16[4,2,131072]{2,1,0:T(2,128)(2,1)}), bf16[4,2,131072]{2,1,0:T(2,128)(2,1)S(1)}, u32[]{:S(2)}, u32[]{:S(2)}) async-start(bf16[4,2,131072]{2,1,0:T(2,128)(2,1)} %reshape.158), calls=%async_computation.1 | async-start | bytes 4194304 | tf_op jit(solution)/shard_map/all_to_all | solution.py:56
  267.8 30.7 %all-to-all-start.2 = ((bf16[4,2,131072]{2,1,0:T(2,128)(2,1)}), bf16[4,2,131072]{2,1,0:T(2,128)(2,1)}, u32[]{:S(2)}, u32[]{:S(2)}) async-start(bf16[4,2,131072]{2,1,0:T(2,128)(2,1)} %reshape.160), calls=%async_computation.2 | async-start | bytes 4194304 | tf_op jit(solution)/shard_map/all_to_all | solution.py:59
  272.7 4.1 copy-start.4
  283.5 20.7 %copy-start.8 = (bf16[4,8,64,64]{3,2,1,0:T(8,128)(2,1)S(1)}, bf16[4,8,64,64]{3,2,1,0:T(8,128)(2,1)}, u32[]{:S(2)}) copy-start(bf16[4,8,64,64]{3,2,1,0:T(8,128)(2,1)} %param.15) | copy-start | bytes 786436
  304.2 10.8 %copy-start.5 = (bf16[4,8,64,64]{3,2,1,0:T(8,128)(2,1)S(1)}, bf16[4,8,64,64]{3,2,1,0:T(8,128)(2,1)}, u32[]{:S(2)}) copy-start(bf16[4,8,64,64]{3,2,1,0:T(8,128)(2,1)} %param.16) | copy-start | bytes 786436
  431.3 5.1 copy-start.7
  431.3 5.2 copy-start.6
  431.3 166.5 %all-to-all-start.4 = ((bf16[8,4,64,1792]{3,2,1,0:T(8,128)(2,1)}), bf16[8,4,64,1792]{3,2,1,0:T(8,128)(2,1)}, u32[]{:S(2)}, u32[]{:S(2)}) async-start(bf16[8,4,64,1792]{3,2,1,0:T(8,128)(2,1)} %reshape.120), calls=%async_computation.4 | async-start | bytes 14680064 | tf_op jit(solution)/shard_map/all_to_all | solution.py:84
where the time goes:
time: 621 us; the launch traced here: 616 us
  blocking collectives  357 us (57%)
  local copies, waits for them, and re-layouts  152 us (24%)
  matrix products  50.9 us (8%)
  waiting for transfers between devices  20.2 us (3%)
  other arithmetic  19.9 us (3%)
  starting transfers between devices  13.8 us (2%)
    all_to_all x1, blocking collectives, shards(): lax.all_to_all(outgoing, 'expert', split_axis=0, concat_axis=0, tiled=True)  168 us
    psum x1, blocking collectives, shards(): totals = lax.psum(counts, 'expert')  160 us
    unnamed x26, local copies, waits for them, and re-layouts  33.6 us
    all_to_all x1, blocking collectives, shards(): lax.all_to_all(down_split, 'dp', split_axis=2, concat_axis=2, tiled=True)  28.9 us
    convert_element_type x1, local copies, waits for them, and re-layouts, shards(): expert_out.astype(jnp.bfloat16).reshape(sources, local, slots, width_here)  23.1 us
    reshape x1, local copies, waits for them, and re-layouts, shards(): received.reshape(sources, local, slots, blocks_here, block_width)  17.4 us
    reshape x1, local copies, waits for them, and re-layouts, shards(): expert_out.astype(jnp.bfloat16).reshape(sources, local, slots, width_here)  15.2 us
    all_to_all x1, waiting for transfers between devices, shards(): lax.all_to_all(up_low.astype(jnp.bfloat16).reshape(layout), 'dp', split_a...  14.9 us
  transfers between devices with their start and end apart: 3, of which 2 were waited for; matrix products, arithmetic and copies ran while one was open for 5% of the time, Pallas kernels for 0%

commit v1 on v0

--- a/solution.py
+++ b/solution.py
@@ -91,9 +91,115 @@
     return (moe_output, expert_load)
 
 
+def spread_weights(dp_count, gate_first, up_first, gate_second, up_second, down_first, down_second):
+    per_dev, blocks_here, block_width, rank_size = gate_first.shape
+    rank_here, block_count = gate_second.shape[1:3]
+    halves = 2
+    half = blocks_here // halves
+    same_block = jnp.eye(half, dtype=jnp.bfloat16)
+    same_rank = jnp.eye(rank_here, dtype=jnp.bfloat16)
+    same_side = jnp.eye(2, dtype=jnp.bfloat16)
+    same_out = jnp.eye(blocks_here, dtype=jnp.bfloat16)
+    first = jnp.stack([gate_first, up_first], axis=4).reshape(
+        per_dev, halves, half, block_width, dp_count, rank_here, 2
+    )
+    first = jnp.einsum("ehjfqcg,jk->ehjfqgck", first, same_block).reshape(
+        per_dev, halves, half * block_width, dp_count * 2 * rank_here * half
+    )
+    second = jnp.stack([gate_second, up_second], axis=1).reshape(
+        per_dev, 2, rank_here, dp_count, halves, half, block_count
+    )
+    second = jnp.einsum("egcphjm,gk,cd->ephgcjkdm", second, same_side, same_rank).reshape(
+        per_dev, 2 * rank_here * block_count, 2 * rank_here * block_count
+    )
+    third = down_first.reshape(per_dev, rank_here, block_count, dp_count, blocks_here)
+    third = jnp.einsum("ecmpn,cd->ecmpdn", third, same_rank).reshape(
+        per_dev, rank_here * block_count, rank_here * block_count
+    )
+    fourth = down_second.reshape(per_dev, blocks_here, dp_count, rank_here, block_width)
+    fourth = jnp.einsum("enqcf,nk->eqcnkf", fourth, same_out).reshape(
+        per_dev, rank_size * blocks_here, blocks_here * block_width
+    )
+    return first, second, third, fourth
+
+
+def gathered(tokens, routes, route_weight, *weights):
+    tok_rows, width_here = tokens.shape
+    top_k = routes.shape[1]
+    groups = lax.axis_size("expert")
+    dp_count = lax.axis_size("dp")
+    per_dev, blocks_here = weights[0].shape[:2]
+    experts = per_dev * groups
+    capacity = 2 * tok_rows * top_k // experts
+    tokens_all = lax.all_gather(tokens, "expert")
+    both = jnp.concatenate([routes.astype(jnp.float32), route_weight], axis=1)
+    both = lax.all_gather(both, "expert")
+    first, second, third, fourth = spread_weights(dp_count, *weights)
+    halves = first.shape[1]
+    mine = lax.axis_index("expert") * per_dev + jnp.arange(per_dev)
+    named = both[:, :, :top_k, None] == mine.astype(jnp.float32)
+    hit = jnp.any(named, axis=2)
+    weight = jnp.sum(jnp.where(named, both[:, :, top_k:, None], 0.0), axis=2)
+    ahead = jnp.tril(jnp.ones((tok_rows, tok_rows), jnp.bfloat16), -1)
+    position = jnp.einsum(
+        "tu,gue->gte", ahead, hit.astype(jnp.bfloat16), preferred_element_type=jnp.float32
+    )
+    position = jnp.where(hit, position, -1.0)
+    slot = jnp.arange(capacity, dtype=jnp.float32)
+    chosen = position[:, :, :, None] == slot
+    dispatch = chosen.astype(jnp.bfloat16).reshape(groups, tok_rows, per_dev * capacity)
+    combine = jnp.where(chosen, weight[:, :, :, None], 0.0).astype(jnp.bfloat16)
+    combine = combine.reshape(groups, tok_rows, per_dev * capacity)
+    rows = jnp.einsum(
+        "gts,gtd->gsd", dispatch, tokens_all, preferred_element_type=jnp.float32
+    ).astype(jnp.bfloat16)
+    rows = rows.reshape(groups, per_dev, capacity, halves, width_here // halves)
+    low = jnp.einsum(
+        "geshk,ehkn->ehgsn", rows, first, preferred_element_type=jnp.float32
+    ).astype(jnp.bfloat16)
+    low = low.reshape(low.shape[:4] + (dp_count, -1))
+    low = lax.all_to_all(low.transpose(4, 0, 1, 2, 3, 5), "dp", 0, 0, tiled=True)
+    high = jnp.einsum(
+        "pehgsk,ephkn->egsn",
+        low,
+        second.reshape(per_dev, dp_count, halves, -1, second.shape[2]),
+        preferred_element_type=jnp.float32,
+    )
+    gate_high, up_high = jnp.split(high, 2, axis=-1)
+    activated = (jax.nn.silu(gate_high) * up_high).astype(jnp.bfloat16)
+    down = jnp.einsum(
+        "egsk,ekn->egsn", activated, third, preferred_element_type=jnp.float32
+    ).astype(jnp.bfloat16)
+    down = down.reshape(down.shape[:3] + (dp_count, -1))
+    down = lax.all_to_all(down.transpose(3, 0, 1, 2, 4), "dp", 0, 0, tiled=True)
+    out = jnp.einsum(
+        "qegsk,eqkd->gesd",
+        down,
+        fourth.reshape(per_dev, dp_count, -1, width_here),
+        preferred_element_type=jnp.float32,
+    ).astype(jnp.bfloat16)
+    partial = jnp.einsum(
+        "gts,gsd->gtd",
+        combine,
+        out.reshape(groups, per_dev * capacity, width_here),
+        preferred_element_type=jnp.float32,
+    ).astype(jnp.bfloat16)
+    moe_output = lax.psum_scatter(partial, "expert", scatter_dimension=0)
+    counts = jnp.sum(hit.astype(jnp.float32), axis=(0, 1))
+    expert_load = counts * experts / (tok_rows * groups * top_k)
+    return (moe_output, expert_load)
+
+
+def chosen_plan(tokens, routes, *rest):
+    groups = lax.axis_size("expert")
+    if groups <= 2 * routes.shape[1]:
+        return gathered(tokens, routes, *rest)
+    return shards(tokens, routes, *rest)
+
+
 def solution(mesh):
     return jax.shard_map(
-        shards,
+        chosen_plan,
         mesh=mesh,
         in_specs=(
             P("expert", "dp"),

time: 621 us -> 324 us (0.52)
  blocking collectives: 357 us -> 32.9 us
  waiting for transfers between devices: 20.2 us -> 109 us
  local copies, waits for them, and re-layouts: 152 us -> 93.4 us
  between operations: 1.38 us -> 14.2 us
  matrix products: 50.9 us -> 40.3 us
    all_to_all x2 -> x0, blocking collectives: 197 us -> none  [the longest x1 168 us: shards(): lax.all_to_all(outgoing, 'expert', split_axis=0, concat_axis=0, tiled=True)]
    psum x1 -> x0, blocking collectives: 160 us -> none  [shards(): totals = lax.psum(counts, 'expert')]
    reduce_scatter x0 -> x1, waiting for transfers between devices: none -> 78.3 us  [gathered(): moe_output = lax.psum_scatter(partial, 'expert', scatter_dimension=0)]
    another operation x2 -> x4, local copies, waits for them, and re-layouts: 0.08 us -> 38.6 us  [the longest x1 22.6 us: gathered(): second.reshape(per_dev, dp_count, halves, -1, second.shape[2])]
    unnamed x26 -> x11, local copies, waits for them, and re-layouts: 33.6 us -> 0.05 us
    all_gather x0 -> x1, blocking collectives: none -> 32.9 us  [gathered(): both = lax.all_gather(both, 'expert')]
    convert_element_type x2 -> x1, local copies, waits for them, and re-layouts: 29.8 us -> 3.88 us  [gathered(): out = jnp.einsum('qegsk,eqkd->gesd', down, fourth.reshape(per_dev, dp_cou...]
    gather x2 -> x0, local copies, waits for them, and re-layouts: 22.6 us -> none  [the longest x1 12 us: shards(): picked = jnp.take(returned, slot_index, axis=0).astype(jnp.float32)]
  transfers between devices with their start and end apart: 3 -> 4, of which waited for: 2 -> 4; matrix products, arithmetic and copies ran while one was open for 5% -> 26% of each run, Pallas kernels for 0% -> 0%
where the time goes in v1:
time: 324 us; the launch traced here: 322 us
  waiting for transfers between devices  109 us (34%)
  local copies, waits for them, and re-layouts  93.4 us (29%)
  matrix products  40.3 us (12%)
  blocking collectives  32.9 us (10%)
  other arithmetic  23.5 us (7%)
  between operations  14.2 us (4%)
  starting transfers between devices  8.99 us (3%)
    reduce_scatter x1, waiting for transfers between devices, gathered(): moe_output = lax.psum_scatter(partial, 'expert', scatter_dimension=0)  78.3 us
    all_gather x1, blocking collectives, gathered(): both = lax.all_gather(both, 'expert')  32.9 us
    another operation x1, local copies, waits for them, and re-layouts, gathered(): second.reshape(per_dev, dp_count, halves, -1, second.shape[2])  22.6 us
    all_gather x1, waiting for transfers between devices, gathered(): tokens_all = lax.all_gather(tokens, 'expert')  16.1 us
    another operation x1, local copies, waits for them, and re-layouts, gathered(): fourth.reshape(per_dev, dp_count, -1, width_here)  15.2 us
    reshape x1, local copies, waits for them, and re-layouts, gathered(): rows = rows.reshape(groups, per_dev, capacity, halves, width_here // halves)  14.6 us
    reshape x1, local copies, waits for them, and re-layouts, spread_weights(): jnp.einsum('ehjfqcg,jk->ehjfqgck', first, same_block)  14.4 us
    reshape x2, local copies, waits for them, and re-layouts, gathered(): low = low.reshape(low.shape[:4] + (dp_count, -1))  12.3 us
  transfers between devices with their start and end apart: 4, of which 4 were waited for; matrix products, arithmetic and copies ran while one was open for 26% of the time, Pallas kernels for 0%

profile of v1, /device:TPU:0, one launch (start us, length us, event | category | flops | bytes accessed | tf_op | source)
XLA Modules:
  0.0 322.0 jit_solution(13767979106421051806)
XLA Ops:
  7.2 0.7 all-gather.4.cloned.1.call-update
  7.9 0.7 convert_element_type.44
  8.6 0.7 pad_maximum_fusion
  9.3 32.9 %all-gather = f32[1024,16]{0,1:T(8,128)S(1)} all-gather(f32[128,16]{0,1:T(8,128)S(1)} %pad_maximum_fusion), channel_id=2, replica_groups=mesh['dp'=4,'expert'=8] {'expert'}, dimensions={0}, use_global_device_ids=true | all-gather | bytes 73728 | tf_op jit(solution)/shard_map/all_gather | solution.py:136
  42.7 1.4 maximum_bitcast_fusion
  44.2 0.7 copy.61
  44.9 3.8 %multiply_bitcast_fusion.1 = bf16[4,2,8,112,4,2,8,8]{3,2,7,6,5,4,1,0:T(8,128)(2,1)} fusion(bf16[8,4,2,112,4,8,2]{3,0,5,6,4,2,1:T(8,128)(2,1)S(1)} %copy.61, bf16[8,8]{0,1:T(8,128)(2,1)S(1)} %fusion.35), kind=kLoop, calls=%fused_computation.5 | loop fusion | flops 3670016 | bytes 8257664 | tf_op jit(solution)/shard_map/ehjfqcg,jk->ehjfqgck/transpose | solution.py:106
  48.7 14.4 %reshape.61 = bf16[4,2,896,512]{2,3,1,0:T(8,128)(2,1)} reshape(bf16[4,2,8,112,4,2,8,8]{3,2,7,6,5,4,1,0:T(8,128)(2,1)} %multiply_bitcast_fusion.1) | data formatting | bytes 14680064 | tf_op jit(solution)/shard_map/reshape | solution.py:106
  63.4 16.1 %all-gather.4.cloned.1.call-done = bf16[1024,1792]{1,0:T(8,128)(2,1)} async-done(((bf16[128,1792]{1,0:T(8,128)(2,1)}), bf16[1024,1792]{1,0:T(8,128)(2,1)}) %all-gather.4.cloned.1.call-update) | async-done | bytes 3670032 | tf_op jit(solution)/shard_map/all_gather | solution.py:134
  79.4 7.0 %convolution_convert_fusion = bf16[8,256,1792]{2,1,0:T(8,128)(2,1)} fusion(pred[8,128,256]{1,2,0:T(32,128)(4,1)S(1)} %bitcast_compare_fusion, bf16[8,128,1792]{2,1,0:T(8,128)(2,1)} %bitcast.115), kind=kOutput, calls=%fused_computation.13 | convolution fusion | flops 943194112 | bytes 11272192 | tf_op jit(solution)/shard_map/gts,gtd->gsd/dot_general | solution.py:153
  86.5 14.6 %reshape.60 = bf16[8,4,64,2,896]{4,3,2,1,0:T(2,128)(2,1)} reshape(bf16[8,256,1792]{2,1,0:T(8,128)(2,1)} %convolution_convert_fusion) | data formatting | bytes 14680064 | tf_op jit(solution)/shard_map/reshape | solution.py:156
  101.1 11.7 %fusion.11 = bf16[4,2,8,64,512]{4,3,2,1,0:T(8,128)(2,1)} fusion(bf16[4,2,896,512]{2,3,1,0:T(8,128)(2,1)} %reshape.61, bf16[8,4,64,2,896]{4,3,2,1,0:T(2,128)(2,1)} %reshape.60), kind=kOutput, calls=%fused_computation.19 | convolution fusion | flops 3760193536 | bytes 18874368 | tf_op jit(solution)/shard_map/geshk,ehkn->ehgsn/dot_general | solution.py:157
  112.7 6.9 %reshape.62 = bf16[4,2,8,64,4,128]{5,4,3,2,1,0:T(4,128)(2,1)} reshape(bf16[4,2,8,64,512]{4,3,2,1,0:T(8,128)(2,1)} %fusion.11) | data formatting | bytes 8388608 | tf_op jit(solution)/shard_map/reshape | solution.py:160
  119.7 5.4 %copy.111 = bf16[4,2,8,64,4,128]{5,3,1,2,0,4:T(8,128)(2,1)} copy(bf16[4,2,8,64,4,128]{5,4,3,2,1,0:T(4,128)(2,1)} %reshape.62) | data formatting | bytes 8388608 | tf_op jit(solution)/shard_map/reshape | solution.py:160
  125.0 5.1 %all-to-all-start = ((bf16[4,4,2,8,64,128]{5,4,2,3,1,0:T(8,128)(2,1)}), bf16[4,4,2,8,64,128]{5,4,2,3,1,0:T(8,128)(2,1)}, u32[]{:S(2)}, u32[]{:S(2)}) async-start(bf16[4,4,2,8,64,128]{5,4,2,3,1,0:T(8,128)(2,1)} %bitcast.113), calls=%async_computation | async-start | bytes 8388608 | tf_op jit(solution)/shard_map/all_to_all | solution.py:161
  130.3 9.1 %multiply_bitcast_fusion = bf16[4,4,2,2,8,8,2,8,64]{8,7,6,5,4,3,2,0,1:T(8,128)(2,1)} fusion(bf16[2,8,8,2]{2,3,1,0:T(2,128)(2,1)S(1)} %multiply_bitcast_fusion.4, bf16[4,1,8,4,2,8,64]{6,5,4,3,2,0,1:T(8,128)(2,1)S(1)} %bitcast.117, bf16[4,1,8,4,2,8,64]{6,5,4,3,2,0,1:T(8,128)(2,1)S(1)} %bitcast.118), kind=kLoop, calls=%fused_computation | loop fusion | flops 17039360 | bytes 8913408 | tf_op jit(solution)/shard_map/egcphjm,gk,cd->ephgcjkdm/transpose | solution.py:112
  139.4 22.6 %reshape.72 = bf16[4,4,2,128,1024,1]{4,3,2,0,1,5:T(8,128)(2,1)} reshape(bf16[4,4,2,2,8,8,2,8,64]{8,7,6,5,4,3,2,0,1:T(8,128)(2,1)} %multiply_bitcast_fusion) | data formatting | bytes 16777216 | tf_op jit(solution)/shard_map/reshape;reshape | solution.py:165
  162.4 2.3 multiply_bitcast_fusion.3
  164.7 5.4 %reshape.65 = bf16[4,512,512]{1,2,0:T(8,128)(2,1)S(1)} reshape(bf16[4,8,64,4,8,16]{2,1,5,4,3,0:T(8,128)(2,1)} %multiply_bitcast_fusion.3) | data formatting | bytes 4194304 | tf_op jit(solution)/shard_map/reshape | solution.py:116
  170.0 8.1 %all-to-all-done = bf16[4,4,2,8,64,128]{5,4,2,3,1,0:T(8,128)(2,1)} async-done(((bf16[4,4,2,8,64,128]{5,4,2,3,1,0:T(8,128)(2,1)}), bf16[4,4,2,8,64,128]{5,4,2,3,1,0:T(8,128)(2,1)}, u32[]{:S(2)}, u32[]{:S(2)}) %all-to-all-start) | async-done | bytes 4194336 | tf_op jit(solution)/shard_map/all_to_all | solution.py:161
  178.1 7.5 %fusion = f32[4,8,64,1024,1,1]{3,2,4,1,0,5:T(8,128)S(1)} fusion(bf16[4,4,2,8,64,128]{5,4,2,3,1,0:T(8,128)(2,1)} %all-to-all-done, bf16[4,4,2,128,1024,1]{4,3,2,0,1,5:T(8,128)(2,1)} %reshape.72), kind=kOutput, calls=%fused_computation.2 | convolution fusion | flops 4294967296 | bytes 20971520 | tf_op jit(solution)/shard_map/pehgsk,ephkn->egsn/dot_general | solution.py:162
  185.7 1.7 copy.110
  187.3 1.6 convert_bitcast_fusion
  189.0 1.9 copy.112
  190.9 3.6 %all-to-all-start.1 = ((bf16[4,4,8,64,128]{4,3,2,1,0:T(8,128)(2,1)}), bf16[4,4,8,64,128]{4,3,2,1,0:T(8,128)(2,1)S(1)}, u32[]{:S(2)}, u32[]{:S(2)}) async-start(bf16[4,4,8,64,128]{4,3,2,1,0:T(8,128)(2,1)} %bitcast.111), calls=%async_computation.1 | async-start | bytes 4194304 | tf_op jit(solution)/shard_map/all_to_all | solution.py:174
  195.0 4.1 %multiply_bitcast_fusion.2 = bf16[4,4,8,16,16,112]{5,4,3,2,1,0:T(8,128)(2,1)} fusion(bf16[16,4,4,8,112]{4,0,3,2,1:T(8,128)(2,1)S(1)} %copy.60, bf16[16,16]{1,0:T(8,128)(2,1)S(1)} %fusion.34), kind=kLoop, calls=%fused_computation.6 | loop fusion | flops 3670016 | bytes 7799296 | tf_op jit(solution)/shard_map/enqcf,nk->eqcnkf/transpose | solution.py:120
  199.1 15.2 %reshape.75 = bf16[4,4,128,1792,1]{3,2,1,0,4:T(8,128)(2,1)} reshape(bf16[4,4,8,16,16,112]{5,4,3,2,1,0:T(8,128)(2,1)} %multiply_bitcast_fusion.2) | data formatting | bytes 14680064 | tf_op jit(solution)/shard_map/reshape;reshape | solution.py:178
  214.7 5.5 %all-to-all-done.1 = bf16[4,4,8,64,128]{4,3,2,1,0:T(8,128)(2,1)S(1)} async-done(((bf16[4,4,8,64,128]{4,3,2,1,0:T(8,128)(2,1)}), bf16[4,4,8,64,128]{4,3,2,1,0:T(8,128)(2,1)S(1)}, u32[]{:S(2)}, u32[]{:S(2)}) %all-to-all-start.1) | async-done | bytes 2097184 | tf_op jit(solution)/shard_map/all_to_all | solution.py:174
  220.1 9.2 %fusion.2 = bf16[8,4,64,1792]{3,2,0,1:T(8,128)(2,1)} fusion(bf16[4,4,128,1792,1]{3,2,1,0,4:T(8,128)(2,1)} %reshape.75, bf16[4,4,8,64,128]{4,3,2,1,0:T(8,128)(2,1)S(1)} %all-to-all-done.1), kind=kOutput, calls=%fused_computation.7 | convolution fusion | flops 3761766400 | bytes 16777216 | tf_op jit(solution)/shard_map/qegsk,eqkd->gesd/dot_general | solution.py:175
  229.3 3.9 %copy.74 = bf16[8,4,64,1792]{3,2,1,0:T(8,128)(2,1)S(1)} copy(bf16[8,4,64,1792]{3,2,0,1:T(8,128)(2,1)} %fusion.2) | data formatting | bytes 14680064 | tf_op jit(solution)/shard_map/convert_element_type | solution.py:180
  233.2 3.0 convolution_convert_fusion.1
  236.9 78.3 %reduce-scatter.2.cloned.1.call-done = bf16[1,128,1792]{2,1,0:T(8,128)(2,1)} async-done(((bf16[8,128,1792]{2,1,0:T(8,128)(2,1)}), bf16[1,128,1792]{2,1,0:T(8,128)(2,1)}) %reduce-scatter.2.cloned.1.call-update) | async-done | bytes 458768 | tf_op jit(solution)/shard_map/reduce_scatter | solution.py:187
  (34 shorter events, 2.7 us)
Async XLA Ops:
  7.2 72.3 %all-gather.4.cloned.1.call-start = ((), (), s32[]{:S(2)}) async-start(), calls=%async_computation.4 | async-start | bytes 4128768 | tf_op jit(solution)/shard_map/all_gather | solution.py:134
  119.7 10.6 %copy-start = (bf16[4,8,64,64]{3,2,1,0:T(8,128)(2,1)S(1)}, bf16[4,8,64,64]{3,2,1,0:T(8,128)(2,1)}, u32[]{:S(2)}) copy-start(bf16[4,8,64,64]{3,2,1,0:T(8,128)(2,1)} %param.15) | copy-start | bytes 786436
  119.7 10.6 %copy-start.1 = (bf16[4,8,64,64]{3,2,1,0:T(8,128)(2,1)S(1)}, bf16[4,8,64,64]{3,2,1,0:T(8,128)(2,1)}, u32[]{:S(2)}) copy-start(bf16[4,8,64,64]{3,2,1,0:T(8,128)(2,1)} %param.14) | copy-start | bytes 786436
  125.0 53.1 %all-to-all-start = ((bf16[4,4,2,8,64,128]{5,4,2,3,1,0:T(8,128)(2,1)}), bf16[4,4,2,8,64,128]{5,4,2,3,1,0:T(8,128)(2,1)}, u32[]{:S(2)}, u32[]{:S(2)}) async-start(bf16[4,4,2,8,64,128]{5,4,2,3,1,0:T(8,128)(2,1)} %bitcast.113), calls=%async_computation | async-start | bytes 8388608 | tf_op jit(solution)/shard_map/all_to_all | solution.py:161
  139.4 22.6 %copy-start.2 = (bf16[4,8,64,64]{3,2,1,0:T(8,128)(2,1)S(1)}, bf16[4,8,64,64]{3,2,1,0:T(8,128)(2,1)}, u32[]{:S(2)}) copy-start(bf16[4,8,64,64]{3,2,1,0:T(8,128)(2,1)} %param.16) | copy-start | bytes 786436
  189.0 5.8 %copy-start.3 = (bf16[4,16,32,112]{3,2,1,0:T(8,128)(2,1)S(1)}, bf16[4,16,32,112]{3,2,1,0:T(8,128)(2,1)}, u32[]{:S(2)}) copy-start(bf16[4,16,32,112]{3,2,1,0:T(8,128)(2,1)} %param.17) | copy-start | bytes 1376260
  190.9 29.2 %all-to-all-start.1 = ((bf16[4,4,8,64,128]{4,3,2,1,0:T(8,128)(2,1)}), bf16[4,4,8,64,128]{4,3,2,1,0:T(8,128)(2,1)S(1)}, u32[]{:S(2)}, u32[]{:S(2)}) async-start(bf16[4,4,8,64,128]{4,3,2,1,0:T(8,128)(2,1)} %bitcast.111), calls=%async_computation.1 | async-start | bytes 4194304 | tf_op jit(solution)/shard_map/all_to_all | solution.py:174
  194.5 120.6 %reduce-scatter.2.cloned.1.call-start = ((), (), s32[]{:S(2)}) async-start(), calls=%async_computation.3 | async-start | bytes 4128768 | tf_op jit(solution)/shard_map/reduce_scatter | solution.py:187
Sparse Core Ops, SparseCore 0:
  10.2 69.2 all-gather.3
  236.3 78.7 reduce-scatter.1

commit v2 on v0

--- a/solution.py
+++ b/solution.py
@@ -1,7 +1,15 @@
+import functools
+
 import jax
 import jax.numpy as jnp
 from jax import lax
+from jax.experimental import pallas as pl
+from jax.experimental.pallas import tpu as pltpu
 from jax.sharding import PartitionSpec as P
+
+F32 = jnp.float32
+BF16 = jnp.bfloat16
+MESH = pl.DeviceIdType.MESH
 
 
 def shards(
@@ -91,9 +99,425 @@
     return (moe_output, expert_load)
 
 
+def xor(a, b, count):
+    total, bit = 0, 1
+    while bit < count:
+        total = total + bit * ((a // bit + b // bit) % 2)
+        bit *= 2
+    return total
+
+
+def dot(a, b):
+    return jnp.dot(a, b, preferred_element_type=F32)
+
+
+def ones_at(shape, row_to_column):
+    lead = shape[:-1]
+    target = row_to_column(*[lax.broadcasted_iota(jnp.int32, shape, d) for d in range(len(lead))])
+    column = lax.broadcasted_iota(jnp.int32, shape, len(lead))
+    hit = jnp.where(column == target, F32(1), F32(0))
+    return hit.reshape(-1, shape[-1]).astype(BF16)
+
+
+def expert_kernel(
+    sizes,
+    tok, meta, gf, uf, gs, us, df, ds,
+    out, counts,
+    tok_all, meta_all, w1, w2, w3, w4, wide, rows, low_out, low_in, down_out, down_in,
+    combine, made, own_part, x_out, x_in, z_out, z_in,
+    tok_z, tok_x, tok_in, meta_z, meta_x, meta_in, low_s, low_r, down_s, down_r,
+    local_s, x_s, x_r, z_s, z_r,
+):
+    groups, dp, top_k, cap = sizes
+    per_dev, blocks, width, rank = gf.shape
+    rank_here, block_count = gs.shape[1:3]
+    tok_rows, features = tok.shape
+    half = blocks // 2
+    half_width = half * width
+    chunk = 2 * rank_here * half
+    pieces = 2 * dp
+    hidden = rank_here * block_count
+    slots = per_dev * cap
+    nz = groups // 2
+    d = lax.axis_index("dp")
+    g = lax.axis_index("expert")
+    z, x = g // 2, g % 2
+
+    def at_dp(r):
+        return (xor(d, r, dp), g)
+
+    partner = (d, z * 2 + (1 - x))
+
+    def at_z(k):
+        return (d, xor(z, k, nz) * 2 + x)
+
+    def remote(src, dst, send, recv, to):
+        return pltpu.make_async_remote_copy(
+            src_ref=src, dst_ref=dst, send_sem=send, recv_sem=recv,
+            device_id=to, device_id_type=MESH,
+        )
+
+    barrier = pltpu.get_barrier_semaphore()
+    peers = [at_dp(r) for r in range(1, dp)] + [partner] + [at_z(k) for k in range(1, nz)]
+    for peer in peers:
+        pl.semaphore_signal(barrier, inc=1, device_id=peer, device_id_type=MESH)
+    pl.semaphore_wait(barrier, len(peers))
+
+    def slot_of(k, b):
+        return xor(z, k, nz) * 2 + (x + b) % 2
+
+    def z_copies(k):
+        return (
+            remote(meta, meta_all.at[g], meta_z.at[k], meta_in.at[g], at_z(k)),
+            remote(tok, tok_all.at[g], tok_z.at[k], tok_in.at[g], at_z(k)),
+        )
+
+    def x_copies(k):
+        slot = slot_of(k, 0)
+        return (
+            remote(meta_all.at[slot], meta_all.at[slot], meta_x.at[k], meta_in.at[slot], partner),
+            remote(tok_all.at[slot], tok_all.at[slot], tok_x.at[k], tok_in.at[slot], partner),
+        )
+
+    def own_x_copies():
+        return (
+            remote(meta, meta_all.at[g], meta_x.at[0], meta_in.at[g], partner),
+            remote(tok, tok_all.at[g], tok_x.at[0], tok_in.at[g], partner),
+        )
+
+    def wait_slot(slot):
+        remote(meta, meta_all.at[slot], meta_x.at[0], meta_in.at[slot], partner).wait_recv()
+        remote(tok, tok_all.at[slot], tok_x.at[0], tok_in.at[slot], partner).wait_recv()
+
+    for k in range(1, nz):
+        for copy in z_copies(k):
+            copy.start()
+    for copy in own_x_copies():
+        copy.start()
+    tok_all[g] = tok[...]
+    meta_all[g] = meta[...]
+    counts[...] = jnp.zeros_like(counts)
+
+    @pl.loop(0, blocks)
+    def _(b):
+        j = b % half
+        places = [
+            ones_at(
+                (dp, rank_here, dp * chunk),
+                lambda q, c: q * chunk + side * (chunk // 2) + c * half + j,
+            )
+            for side in range(2)
+        ]
+        value = dot(gf[:, b].reshape(-1, rank), places[0])
+        value += dot(uf[:, b].reshape(-1, rank), places[1])
+        w1[:, b] = value.astype(BF16).reshape(per_dev, width, dp * chunk)
+
+    def spread_rest():
+        wide[...] = jnp.zeros_like(wide)
+
+        @pl.loop(0, per_dev)
+        def _(e):
+            for side, ref in enumerate((gs, us)):
+                for c in range(rank_here):
+                    lane = (c * block_count) % 128
+                    value = dot(ref[e, c], ones_at((block_count, 128), lambda r: r + lane))
+                    row = side * (chunk // 2) + c * half
+                    start = side * hidden + c * block_count - lane
+                    wide[:, row : row + half, start : start + 128] = value.reshape(
+                        pieces, half, 128
+                    )
+            for piece in range(pieces):
+                w2[e, piece] = wide[piece].astype(BF16)
+
+        @pl.loop(0, rank_here)
+        def _(c):
+            place = ones_at((block_count, hidden), lambda r: r * rank_here + c)
+            value = dot(df[:, c].reshape(-1, block_count), place)
+            w3[:, c] = value.astype(BF16).reshape(per_dev, block_count, hidden)
+
+        wide[...] = jnp.zeros_like(wide)
+
+        @pl.loop(0, per_dev)
+        def _(e):
+            for n in range(blocks):
+                h = n // half
+                offset = (n % half) * width
+                lane = offset % 128
+                span = -(-(lane + width) // 128) * 128
+                value = dot(ds[e, n], ones_at((width, span), lambda r: r + lane))
+                wide[
+                    h * dp : (h + 1) * dp,
+                    n * rank_here : (n + 1) * rank_here,
+                    offset - lane : offset - lane + span,
+                ] = value.reshape(dp, rank_here, span)
+            for q in range(dp):
+                for h in range(2):
+                    w4[e, q, :, h * half_width : (h + 1) * half_width] = wide[
+                        h * dp + q, :, :half_width
+                    ].astype(BF16)
+
+    def place_of(i):
+        last = groups - 1
+        edge = 1 - (i % last + last - 1) // last
+        return ((i + 1) // 2) % nz, (1 - i % 2 + edge) % 2
+
+    def low_copy(i, r):
+        return remote(
+            low_out.at[i % 2, xor(d, r, dp)], low_in.at[i, d],
+            low_s.at[i % 2, r], low_r.at[i, r], at_dp(r),
+        )
+
+    def down_copy(i, r):
+        return remote(
+            down_out.at[i % 2, xor(d, r, dp)], down_in.at[i, d],
+            down_s.at[i % 2, r], down_r.at[i, r], at_dp(r),
+        )
+
+    def low_local(i):
+        return pltpu.make_async_copy(low_out.at[i % 2, d], low_in.at[i, d], local_s.at[0])
+
+    def down_local(i):
+        return pltpu.make_async_copy(down_out.at[i % 2, d], down_in.at[i, d], local_s.at[1])
+
+    crossing = list(range(dp - 1, 0, -1))
+
+    def stage_a(i):
+        k, b = place_of(i)
+        slot = slot_of(k, b)
+
+        @pl.when(b == 1)
+        def _():
+            wait_slot(slot)
+
+        @pl.when(i >= 2)
+        def _():
+            for r in crossing:
+                low_copy(i, r).wait_send()
+
+        info = meta_all[slot]
+        named_rows, weights = info[:top_k], info[top_k:]
+        line = lax.broadcasted_iota(jnp.int32, (8, tok_rows), 0)
+        hits = jnp.zeros((8, tok_rows), F32)
+        shares = []
+        for e in range(per_dev):
+            named = named_rows == (g * per_dev + e).astype(F32)
+            hit = jnp.max(jnp.where(named, F32(1), F32(0)), axis=0, keepdims=True)
+            hits = hits + jnp.where(line == e, hit, F32(0))
+            shares.append(jnp.sum(jnp.where(named, weights, F32(0)), axis=0, keepdims=True))
+        counts[...] += hits
+        before = lax.broadcasted_iota(jnp.int32, (tok_rows, tok_rows), 0)
+        after = lax.broadcasted_iota(jnp.int32, (tok_rows, tok_rows), 1)
+        ahead = jnp.where(before < after, F32(1), F32(0)).astype(BF16)
+        position = dot(hits.astype(BF16), ahead)
+        position = jnp.where(hits > 0, position, F32(-1)).astype(jnp.int32)
+        slot_row = lax.broadcasted_iota(jnp.int32, (cap, tok_rows), 0)
+        pick, mix = [], []
+        for e in range(per_dev):
+            chosen = slot_row == position[e : e + 1]
+            pick.append(jnp.where(chosen, F32(1), F32(0)))
+            mix.append(jnp.where(chosen, shares[e], F32(0)))
+        pick = jnp.concatenate(pick, axis=0).astype(BF16)
+        combine[i] = jnp.concatenate(mix, axis=0).T.astype(BF16)
+        rows[...] = dot(pick, tok_all[slot]).astype(BF16)
+        for e in range(per_dev):
+            span = slice(e * cap, (e + 1) * cap)
+            for h in range(2):
+                weight = w1[e, h * half : (h + 1) * half].reshape(half_width, dp * chunk)
+                low = dot(rows[span, h * half_width : (h + 1) * half_width], weight).astype(BF16)
+                for q in range(dp):
+                    low_out[i % 2, q, h, span, :] = low[:, q * chunk : (q + 1) * chunk]
+        for r in crossing:
+            low_copy(i, r).start()
+        low_local(i).start()
+        low_local(i).wait()
+
+        @pl.when((i % 2 == 0) & (i // 2 + 1 < nz))
+        def _():
+            after = i // 2 + 1
+            wait_slot(slot_of(after, 0))
+            for copy in x_copies(after):
+                copy.start()
+
+    def stage_b(i):
+        for r in crossing:
+            low_copy(i, r).wait_recv()
+
+        @pl.when(i >= 2)
+        def _():
+            for r in crossing:
+                down_copy(i, r).wait_send()
+
+        for e in range(per_dev):
+            span = slice(e * cap, (e + 1) * cap)
+            low = jnp.concatenate(
+                [low_in[i, p, h, span, :] for p in range(dp) for h in range(2)], axis=1
+            )
+            high = dot(low, w2[e].reshape(pieces * chunk, 2 * hidden))
+            gate, up = high[:, :hidden], high[:, hidden:]
+            activated = (gate / (1 + jnp.exp(-gate)) * up).astype(BF16)
+            down = dot(activated, w3[e].reshape(hidden, hidden)).astype(BF16)
+            for p in range(dp):
+                down_out[i % 2, p, span, :] = down[:, p * chunk : (p + 1) * chunk]
+        for r in crossing:
+            down_copy(i, r).start()
+        down_local(i).start()
+        down_local(i).wait()
+
+    def x_part(k):
+        return remote(x_out.at[k], x_in.at[k], x_s.at[k], x_r.at[k], partner)
+
+    def z_part(k):
+        return remote(z_out.at[k], z_in.at[k], z_s.at[k], z_r.at[k], at_z(k))
+
+    def stage_c(i):
+        k, b = place_of(i)
+        for r in crossing:
+            down_copy(i, r).wait_recv()
+        for e in range(per_dev):
+            span = slice(e * cap, (e + 1) * cap)
+            down = jnp.concatenate([down_in[i, q, span, :] for q in range(dp)], axis=1)
+            made[span, :] = dot(down, w4[e].reshape(dp * chunk, features)).astype(BF16)
+        part = dot(combine[i], made[...]).astype(BF16)
+
+        @pl.when(b == 0)
+        def _():
+            own_part[k] = part
+
+        @pl.when(b == 1)
+        def _():
+            x_out[k] = part
+            x_part(k).start()
+
+    def pass_on(k):
+        x_part(k).wait_recv()
+        z_out[k] = (own_part[k].astype(F32) + x_in[k].astype(F32)).astype(BF16)
+        z_part(k).start()
+
+    @pl.loop(0, groups + 2)
+    def _(step):
+        @pl.when(step < groups)
+        def _():
+            stage_a(step)
+
+        @pl.when(step == 0)
+        def _():
+            spread_rest()
+
+        @pl.when((step >= 1) & (step <= groups))
+        def _():
+            stage_b(step - 1)
+
+        @pl.when((step >= 5) & (step % 2 == 1))
+        def _():
+            pass_on((step - 3) // 2)
+
+        @pl.when(step >= 2)
+        def _():
+            stage_c(step - 2)
+
+    x_part(0).wait_recv()
+    total = own_part[0].astype(F32) + x_in[0].astype(F32)
+    for k in range(1, nz):
+        z_part(k).wait_recv()
+        total += z_in[k].astype(F32)
+    out[...] = total.astype(BF16)
+
+    for k in range(1, nz):
+        for copy in z_copies(k):
+            copy.wait_send()
+        for copy in x_copies(k):
+            copy.wait_send()
+        z_part(k).wait_send()
+    for copy in own_x_copies():
+        copy.wait_send()
+    for k in range(nz):
+        x_part(k).wait_send()
+    for i in (groups - 2, groups - 1):
+        for r in crossing:
+            low_copy(i, r).wait_send()
+            down_copy(i, r).wait_send()
+
+
+def fused(tokens, routes, route_weight, *weights):
+    tok_rows, features = tokens.shape
+    top_k = routes.shape[1]
+    groups = lax.axis_size("expert")
+    dp = lax.axis_size("dp")
+    per_dev, blocks, width, rank = weights[0].shape
+    rank_here, block_count = weights[2].shape[1:3]
+    experts = per_dev * groups
+    cap = 2 * tok_rows * top_k // experts
+    nz = groups // 2
+    chunk = 2 * rank_here * (blocks // 2)
+    hidden = rank_here * block_count
+    slots = per_dev * cap
+    meta = jnp.concatenate([routes.T.astype(F32), route_weight.T], axis=0)
+    vmem = pl.BlockSpec(memory_space=pltpu.VMEM)
+    dma = pltpu.SemaphoreType.DMA
+    out, counts = pl.pallas_call(
+        functools.partial(expert_kernel, (groups, dp, top_k, cap)),
+        out_shape=(
+            jax.ShapeDtypeStruct((tok_rows, features), BF16),
+            jax.ShapeDtypeStruct((8, tok_rows), F32),
+        ),
+        in_specs=[vmem] * 8,
+        out_specs=(vmem, vmem),
+        scratch_shapes=[
+            pltpu.VMEM((groups, tok_rows, features), BF16),
+            pltpu.VMEM((groups, 2 * top_k, tok_rows), F32),
+            pltpu.VMEM((per_dev, blocks, width, dp * chunk), BF16),
+            pltpu.VMEM((per_dev, 2 * dp, chunk, 2 * hidden), BF16),
+            pltpu.VMEM((per_dev, rank_here, block_count, hidden), BF16),
+            pltpu.VMEM((per_dev, dp, chunk, features), BF16),
+            pltpu.VMEM((2 * dp, chunk, 2 * hidden), F32),
+            pltpu.VMEM((slots, features), BF16),
+            pltpu.VMEM((2, dp, 2, slots, chunk), BF16),
+            pltpu.VMEM((groups, dp, 2, slots, chunk), BF16),
+            pltpu.VMEM((2, dp, slots, chunk), BF16),
+            pltpu.VMEM((groups, dp, slots, chunk), BF16),
+            pltpu.VMEM((groups, tok_rows, slots), BF16),
+            pltpu.VMEM((slots, features), BF16),
+            pltpu.VMEM((nz, tok_rows, features), BF16),
+            pltpu.VMEM((nz, tok_rows, features), BF16),
+            pltpu.VMEM((nz, tok_rows, features), BF16),
+            pltpu.VMEM((nz, tok_rows, features), BF16),
+            pltpu.VMEM((nz, tok_rows, features), BF16),
+            dma((nz,)), dma((nz,)), dma((groups,)),
+            dma((nz,)), dma((nz,)), dma((groups,)),
+            dma((2, dp)), dma((groups, dp)), dma((2, dp)), dma((groups, dp)),
+            dma((2,)), dma((nz,)), dma((nz,)), dma((nz,)), dma((nz,)),
+        ],
+        compiler_params=pltpu.CompilerParams(
+            collective_id=0, has_side_effects=True, vmem_limit_bytes=67043328
+        ),
+    )(tokens, meta, *weights)
+    held = jnp.sum(counts, axis=1)[:per_dev]
+    return (out, held * experts / (tok_rows * groups * top_k))
+
+
+def chosen_plan(tokens, routes, route_weight, *weights):
+    groups = lax.axis_size("expert")
+    dp = lax.axis_size("dp")
+    blocks, width = weights[0].shape[1:3]
+    rank_here, block_count = weights[2].shape[1:3]
+    tiled = (
+        tokens.shape[0] % 128 == 0
+        and 2 * rank_here * (blocks // 2) == 128
+        and rank_here == 8
+        and weights[0].shape[0] <= 8
+        and blocks // 2 == 8
+        and block_count == 2 * dp * 8
+        and (blocks // 2 * width) % 128 == 0
+    )
+    powers = groups & (groups - 1) == 0 and dp & (dp - 1) == 0
+    if groups <= 2 * routes.shape[1] and groups >= 4 and dp >= 2 and powers and tiled:
+        return fused(tokens, routes, route_weight, *weights)
+    return shards(tokens, routes, route_weight, *weights)
+
+
 def solution(mesh):
     return jax.shard_map(
-        shards,
+        chosen_plan,
         mesh=mesh,
         in_specs=(
             P("expert", "dp"),

time: 621 us -> 137 us (0.22)
  blocking collectives: 357 us -> 0 us
  local copies, waits for them, and re-layouts: 152 us -> 6.02 us
  Pallas kernels: 0 us -> 125 us
  matrix products: 50.9 us -> 0 us
  waiting for transfers between devices: 20.2 us -> 0 us
  other arithmetic: 19.9 us -> 3.34 us
  starting transfers between devices: 13.8 us -> 0 us
    all_to_all x2 -> x0, blocking collectives: 197 us -> none  [the longest x1 168 us: shards(): lax.all_to_all(outgoing, 'expert', split_axis=0, concat_axis=0, tiled=True)]
    psum x1 -> x0, blocking collectives: 160 us -> none  [shards(): totals = lax.psum(counts, 'expert')]
    pallas_call x0 -> x1, Pallas kernels: none -> 125 us  [fused(): pl.pallas_call(functools.partial(expert_kernel, (groups, dp, top_k, cap))...]
    reshape x6 -> x0, local copies, waits for them, and re-layouts: 51.4 us -> none  [the longest x1 17.4 us: shards(): received.reshape(sources, local, slots, blocks_here, block_width)]
    dot_general x6 -> x0, matrix products: 50.9 us -> none  [the longest x1 11.2 us: shards(): jnp.einsum('aesbf,ebfr->rbeas', split_rows, up_first, preferred_element_t...]
    convert_element_type x2 -> x0, local copies, waits for them, and re-layouts: 29.8 us -> none  [the longest x1 23.1 us: shards(): expert_out.astype(jnp.bfloat16).reshape(sources, local, slots, width_here)]
    unnamed x26 -> x5, local copies, waits for them, and re-layouts: 33.6 us -> 6.02 us
    gather x2 -> x0, local copies, waits for them, and re-layouts: 22.6 us -> none  [the longest x1 12 us: shards(): picked = jnp.take(returned, slot_index, axis=0).astype(jnp.float32)]
  transfers between devices with their start and end apart: 3 -> 0, of which waited for: 2 -> 0; matrix products, arithmetic and copies ran while one was open for 5% -> 0% of each run, Pallas kernels for 0% -> 0%
where the time goes in v2:
time: 137 us; the launch traced here: 135 us
  Pallas kernels  125 us (91%)
  local copies, waits for them, and re-layouts  6.02 us (4%)
  other arithmetic  3.34 us (2%)
    pallas_call x1, Pallas kernels, fused(): pl.pallas_call(functools.partial(expert_kernel, (groups, dp, top_k, cap))...  125 us
    unnamed x5, local copies, waits for them, and re-layouts  6.02 us

profile of v2, /device:TPU:0, one launch (start us, length us, event | category | flops | bytes accessed | tf_op | source)
XLA Modules:
  0.0 135.2 jit_solution(17841358887908150904)
XLA Ops:
  0.6 0.0 copy-start
  0.6 0.7 convert_bitcast_fusion
  1.4 1.3 pad_maximum_fusion.meta
  2.7 2.6 %copy.11.gf = bf16[4,16,112,32]{3,2,1,0:T(8,128)(2,1)} copy(bf16[4,16,112,32]{2,3,1,0:T(8,128)(2,1)} %param.12) | data formatting | bytes 917504 | tf_op args[3]
  5.2 0.0 copy-done
  5.2 1.6 %copy.12.uf = bf16[4,16,112,32]{3,2,1,0:T(8,128)(2,1)} copy(bf16[4,16,112,32]{2,3,1,0:T(8,128)(2,1)S(1)} %copy-done) | data formatting | bytes 917504 | tf_op args[4]
  6.9 125.2 %shard_map.104 = (bf16[128,1792]{1,0:T(8,128)(2,1)}, f32[8,128]{1,0:T(8,128)}) custom-call(bf16[128,1792]{1,0:T(8,128)(2,1)} %tok.1, f32[16,128]{1,0:T(8,128)} %pad_maximum_fusion.meta, bf16[4,16,112,32]{3,2,1,0:T(8,128)(2,1)} %copy.11.gf, bf16[4,16,112,32]{3,2,1,0:T(8,128)(2,1)} %copy.12.uf, bf16[4,8,64,64]{3,2,1,0:T(8,128)(2,1)} %gs.1, ...), custom_call_target="tpu_custom_call" | custom-call | tf_op jit(solution)/shard_map/pallas_call | solution.py:457
  132.1 0.8 reduce_sum.9
  132.9 0.5 slice_multiply_fusion
  133.4 1.8 %copy.14 = bf16[128,1792]{1,0:T(8,128)(2,1)} copy(bf16[128,1792]{1,0:T(8,128)(2,1)} %get-tuple-element.8) | data formatting | bytes 917504
Async XLA Ops:
  0.6 4.6 %copy-start = (bf16[4,16,112,32]{2,3,1,0:T(8,128)(2,1)S(1)}, bf16[4,16,112,32]{2,3,1,0:T(8,128)(2,1)}, u32[]{:S(2)}) copy-start(bf16[4,16,112,32]{2,3,1,0:T(8,128)(2,1)} %param.13) | copy-start | bytes 1376260

commit v3 on v2

--- a/solution.py
+++ b/solution.py
@@ -121,32 +121,32 @@
 
 def expert_kernel(
     sizes,
-    tok, meta, gf, uf, gs, us, df, ds,
-    out, counts,
-    tok_all, meta_all, w1, w2, w3, w4, wide, rows, low_out, low_in, down_out, down_in,
-    combine, made, own_part, x_out, x_in, z_out, z_in,
-    tok_z, tok_x, tok_in, meta_z, meta_x, meta_in, low_s, low_r, down_s, down_r,
-    local_s, x_s, x_r, z_s, z_r,
+    tok, routes, shares_in, gf, uf, gs, df, ds,
+    out, load,
+    tok_all, routes_all, shares_all, gf2, uf2, gs2, df2, ds2,
+    w1, w2, w3, w4, wide, rows, low_out, low_in, down_out, down_in,
+    combine, made, summed, z_out, z_in, counts, counts_in,
+    gather_s, gather_r, weight_s, weight_r, low_s, low_r, down_s, down_r,
+    local_s, count_s, z_s, z_r,
 ):
-    groups, dp, top_k, cap = sizes
-    per_dev, blocks, width, rank = gf.shape
-    rank_here, block_count = gs.shape[1:3]
+    groups, dp, top_k, cap, rank_here, block_count = sizes
+    per_dev, blocks, rank, width = gf.shape
     tok_rows, features = tok.shape
+    experts = per_dev * groups
     half = blocks // 2
     half_width = half * width
     chunk = 2 * rank_here * half
     pieces = 2 * dp
     hidden = rank_here * block_count
-    slots = per_dev * cap
     nz = groups // 2
+    total_steps = 2 * nz
     d = lax.axis_index("dp")
     g = lax.axis_index("expert")
     z, x = g // 2, g % 2
+    partner = (d, z * 2 + (1 - x))
 
     def at_dp(r):
         return (xor(d, r, dp), g)
-
-    partner = (d, z * 2 + (1 - x))
 
     def at_z(k):
         return (d, xor(z, k, nz) * 2 + x)
@@ -163,64 +163,56 @@
         pl.semaphore_signal(barrier, inc=1, device_id=peer, device_id_type=MESH)
     pl.semaphore_wait(barrier, len(peers))
 
-    def slot_of(k, b):
-        return xor(z, k, nz) * 2 + (x + b) % 2
-
-    def z_copies(k):
-        return (
-            remote(meta, meta_all.at[g], meta_z.at[k], meta_in.at[g], at_z(k)),
-            remote(tok, tok_all.at[g], tok_z.at[k], tok_in.at[g], at_z(k)),
-        )
-
-    def x_copies(k):
-        slot = slot_of(k, 0)
-        return (
-            remote(meta_all.at[slot], meta_all.at[slot], meta_x.at[k], meta_in.at[slot], partner),
-            remote(tok_all.at[slot], tok_all.at[slot], tok_x.at[k], tok_in.at[slot], partner),
-        )
-
-    def own_x_copies():
-        return (
-            remote(meta, meta_all.at[g], meta_x.at[0], meta_in.at[g], partner),
-            remote(tok, tok_all.at[g], tok_x.at[0], tok_in.at[g], partner),
-        )
-
-    def wait_slot(slot):
-        remote(meta, meta_all.at[slot], meta_x.at[0], meta_in.at[slot], partner).wait_recv()
-        remote(tok, tok_all.at[slot], tok_x.at[0], tok_in.at[slot], partner).wait_recv()
+    def gather(k):
+        pairs = ((routes, routes_all), (shares_in, shares_all), (tok, tok_all))
+        return [
+            remote(src, dst.at[k], gather_s.at[n, k], gather_r.at[n, k], at_z(k))
+            for n, (src, dst) in enumerate(pairs)
+        ]
+
+    held = (gf, uf, gs, df, ds)
+    swapped = (gf2, uf2, gs2, df2, ds2)
+
+    def swap(n):
+        return remote(held[n], swapped[n], weight_s.at[n], weight_r.at[n], partner)
 
     for k in range(1, nz):
-        for copy in z_copies(k):
+        for copy in gather(k):
             copy.start()
-    for copy in own_x_copies():
-        copy.start()
-    tok_all[g] = tok[...]
-    meta_all[g] = meta[...]
+    for n in range(len(held)):
+        swap(n).start()
+    tok_all[0] = tok[...]
+    routes_all[0] = routes[...]
+    shares_all[0] = shares_in[...]
     counts[...] = jnp.zeros_like(counts)
 
-    @pl.loop(0, blocks)
-    def _(b):
-        j = b % half
-        places = [
-            ones_at(
-                (dp, rank_here, dp * chunk),
-                lambda q, c: q * chunk + side * (chunk // 2) + c * half + j,
+    def spread_first(gate, up):
+        @pl.loop(0, blocks)
+        def _(b):
+            j = b % half
+            place = ones_at(
+                (2, dp, rank_here, dp * chunk),
+                lambda side, q, c: q * chunk + side * (chunk // 2) + c * half + j,
             )
-            for side in range(2)
-        ]
-        value = dot(gf[:, b].reshape(-1, rank), places[0])
-        value += dot(uf[:, b].reshape(-1, rank), places[1])
-        w1[:, b] = value.astype(BF16).reshape(per_dev, width, dp * chunk)
-
-    def spread_rest():
+            for e in range(per_dev):
+                both = jnp.concatenate([gate[e, b], up[e, b]], axis=0)
+                w1[e, b] = lax.dot_general(
+                    both, place, (((0,), (0,)), ((), ())), preferred_element_type=F32
+                ).astype(BF16)
+
+    def spread_middle(second, third):
         wide[...] = jnp.zeros_like(wide)
 
         @pl.loop(0, per_dev)
         def _(e):
-            for side, ref in enumerate((gs, us)):
+            for side in range(2):
                 for c in range(rank_here):
                     lane = (c * block_count) % 128
-                    value = dot(ref[e, c], ones_at((block_count, 128), lambda r: r + lane))
+                    place = ones_at(
+                        (2, block_count, 128),
+                        lambda s, r: jnp.where(s == side, r + lane, -1),
+                    )
+                    value = dot(second[e, c], place)
                     row = side * (chunk // 2) + c * half
                     start = side * hidden + c * block_count - lane
                     wide[:, row : row + half, start : start + 128] = value.reshape(
@@ -231,10 +223,15 @@
 
         @pl.loop(0, rank_here)
         def _(c):
-            place = ones_at((block_count, hidden), lambda r: r * rank_here + c)
-            value = dot(df[:, c].reshape(-1, block_count), place)
+            pairs = rank_here // 2
+            place = ones_at(
+                (2, block_count, hidden),
+                lambda s, r: jnp.where(s == c // pairs, r * rank_here + c, -1),
+            )
+            value = dot(third[:, c % pairs].reshape(-1, 2 * block_count), place)
             w3[:, c] = value.astype(BF16).reshape(per_dev, block_count, hidden)
 
+    def spread_last(fourth):
         wide[...] = jnp.zeros_like(wide)
 
         @pl.loop(0, per_dev)
@@ -244,7 +241,7 @@
                 offset = (n % half) * width
                 lane = offset % 128
                 span = -(-(lane + width) // 128) * 128
-                value = dot(ds[e, n], ones_at((width, span), lambda r: r + lane))
+                value = dot(fourth[e, n], ones_at((width, span), lambda r: r + lane))
                 wide[
                     h * dp : (h + 1) * dp,
                     n * rank_here : (n + 1) * rank_here,
@@ -257,9 +254,8 @@
                     ].astype(BF16)
 
     def place_of(i):
-        last = groups - 1
-        edge = 1 - (i % last + last - 1) // last
-        return ((i + 1) // 2) % nz, (1 - i % 2 + edge) % 2
+        turn = i // nz
+        return turn, (i % nz) * (1 - turn) + (nz - 1 - i % nz) * turn
 
     def low_copy(i, r):
         return remote(
@@ -282,29 +278,29 @@
     crossing = list(range(dp - 1, 0, -1))
 
     def stage_a(i):
-        k, b = place_of(i)
-        slot = slot_of(k, b)
-
-        @pl.when(b == 1)
-        def _():
-            wait_slot(slot)
+        turn, k = place_of(i)
+
+        @pl.when((turn == 0) & (k > 0))
+        def _():
+            for copy in gather(k):
+                copy.wait_recv()
 
         @pl.when(i >= 2)
         def _():
             for r in crossing:
                 low_copy(i, r).wait_send()
 
-        info = meta_all[slot]
-        named_rows, weights = info[:top_k], info[top_k:]
+        base = (z * 2 + (x + turn) % 2) * per_dev
+        named_rows, weights = routes_all[k], shares_all[k]
         line = lax.broadcasted_iota(jnp.int32, (8, tok_rows), 0)
         hits = jnp.zeros((8, tok_rows), F32)
         shares = []
         for e in range(per_dev):
-            named = named_rows == (g * per_dev + e).astype(F32)
+            named = named_rows == base + e
             hit = jnp.max(jnp.where(named, F32(1), F32(0)), axis=0, keepdims=True)
             hits = hits + jnp.where(line == e, hit, F32(0))
             shares.append(jnp.sum(jnp.where(named, weights, F32(0)), axis=0, keepdims=True))
-        counts[...] += hits
+        counts[turn] += hits
         before = lax.broadcasted_iota(jnp.int32, (tok_rows, tok_rows), 0)
         after = lax.broadcasted_iota(jnp.int32, (tok_rows, tok_rows), 1)
         ahead = jnp.where(before < after, F32(1), F32(0)).astype(BF16)
@@ -318,7 +314,7 @@
             mix.append(jnp.where(chosen, shares[e], F32(0)))
         pick = jnp.concatenate(pick, axis=0).astype(BF16)
         combine[i] = jnp.concatenate(mix, axis=0).T.astype(BF16)
-        rows[...] = dot(pick, tok_all[slot]).astype(BF16)
+        rows[...] = dot(pick, tok_all[k]).astype(BF16)
         for e in range(per_dev):
             span = slice(e * cap, (e + 1) * cap)
             for h in range(2):
@@ -330,13 +326,6 @@
             low_copy(i, r).start()
         low_local(i).start()
         low_local(i).wait()
-
-        @pl.when((i % 2 == 0) & (i // 2 + 1 < nz))
-        def _():
-            after = i // 2 + 1
-            wait_slot(slot_of(after, 0))
-            for copy in x_copies(after):
-                copy.start()
 
     def stage_b(i):
         for r in crossing:
@@ -363,108 +352,142 @@
         down_local(i).start()
         down_local(i).wait()
 
-    def x_part(k):
-        return remote(x_out.at[k], x_in.at[k], x_s.at[k], x_r.at[k], partner)
-
     def z_part(k):
         return remote(z_out.at[k], z_in.at[k], z_s.at[k], z_r.at[k], at_z(k))
 
     def stage_c(i):
-        k, b = place_of(i)
+        turn, k = place_of(i)
         for r in crossing:
             down_copy(i, r).wait_recv()
         for e in range(per_dev):
             span = slice(e * cap, (e + 1) * cap)
             down = jnp.concatenate([down_in[i, q, span, :] for q in range(dp)], axis=1)
             made[span, :] = dot(down, w4[e].reshape(dp * chunk, features)).astype(BF16)
-        part = dot(combine[i], made[...]).astype(BF16)
-
-        @pl.when(b == 0)
-        def _():
-            own_part[k] = part
-
-        @pl.when(b == 1)
-        def _():
-            x_out[k] = part
-            x_part(k).start()
-
-    def pass_on(k):
-        x_part(k).wait_recv()
-        z_out[k] = (own_part[k].astype(F32) + x_in[k].astype(F32)).astype(BF16)
-        z_part(k).start()
-
-    @pl.loop(0, groups + 2)
+        part = dot(combine[i], made[...])
+
+        @pl.when(turn == 0)
+        def _():
+            summed[k] = part
+
+        @pl.when((turn == 1) & (k == 0))
+        def _():
+            summed[k] += part
+
+        @pl.when((turn == 1) & (k > 0))
+        def _():
+            z_out[k] = (summed[k] + part).astype(BF16)
+            z_part(k).start()
+
+    count_copy = remote(counts.at[1], counts_in, count_s.at[0], count_s.at[1], partner)
+
+    spread_first(gf, uf)
+
+    @pl.loop(0, total_steps + 2)
     def _(step):
-        @pl.when(step < groups)
+        @pl.when(step == nz)
+        def _():
+            swap(0).wait_recv()
+            swap(1).wait_recv()
+            spread_first(gf2, uf2)
+
+        @pl.when(step < total_steps)
         def _():
             stage_a(step)
 
         @pl.when(step == 0)
         def _():
-            spread_rest()
-
-        @pl.when((step >= 1) & (step <= groups))
+            spread_middle(gs, df)
+            spread_last(ds)
+
+        @pl.when(step == total_steps)
+        def _():
+            count_copy.start()
+
+        @pl.when(step == nz + 1)
+        def _():
+            swap(2).wait_recv()
+            swap(3).wait_recv()
+            spread_middle(gs2, df2)
+
+        @pl.when((step >= 1) & (step <= total_steps))
         def _():
             stage_b(step - 1)
 
-        @pl.when((step >= 5) & (step % 2 == 1))
-        def _():
-            pass_on((step - 3) // 2)
+        @pl.when(step == nz + 2)
+        def _():
+            swap(4).wait_recv()
+            spread_last(ds2)
 
         @pl.when(step >= 2)
         def _():
             stage_c(step - 2)
 
-    x_part(0).wait_recv()
-    total = own_part[0].astype(F32) + x_in[0].astype(F32)
+    count_copy.wait()
+    ones = jnp.ones((8, tok_rows), BF16)
+    held_rows = lax.dot_general(
+        ones, (counts[0] + counts_in[...]).astype(BF16),
+        (((1,), (1,)), ((), ())), preferred_element_type=F32,
+    )
+    load[...] = held_rows[:1, :per_dev] * experts / (tok_rows * groups * top_k)
+
+    total = summed[0]
     for k in range(1, nz):
         z_part(k).wait_recv()
         total += z_in[k].astype(F32)
     out[...] = total.astype(BF16)
 
     for k in range(1, nz):
-        for copy in z_copies(k):
-            copy.wait_send()
-        for copy in x_copies(k):
+        for copy in gather(k):
             copy.wait_send()
         z_part(k).wait_send()
-    for copy in own_x_copies():
-        copy.wait_send()
-    for k in range(nz):
-        x_part(k).wait_send()
-    for i in (groups - 2, groups - 1):
+    for n in range(len(held)):
+        swap(n).wait_send()
+    for i in (total_steps - 2, total_steps - 1):
         for r in crossing:
             low_copy(i, r).wait_send()
             down_copy(i, r).wait_send()
 
 
-def fused(tokens, routes, route_weight, *weights):
+def fused(
+    tokens, routes, route_weight,
+    gate_first, up_first, gate_second, up_second, down_first, down_second,
+):
     tok_rows, features = tokens.shape
     top_k = routes.shape[1]
     groups = lax.axis_size("expert")
     dp = lax.axis_size("dp")
-    per_dev, blocks, width, rank = weights[0].shape
-    rank_here, block_count = weights[2].shape[1:3]
+    per_dev, blocks, width, rank = gate_first.shape
+    rank_here, block_count = gate_second.shape[1:3]
     experts = per_dev * groups
     cap = 2 * tok_rows * top_k // experts
     nz = groups // 2
+    steps = 2 * nz
     chunk = 2 * rank_here * (blocks // 2)
     hidden = rank_here * block_count
     slots = per_dev * cap
-    meta = jnp.concatenate([routes.T.astype(F32), route_weight.T], axis=0)
+    pairs = rank_here // 2
+    factors = (
+        gate_first.swapaxes(2, 3),
+        up_first.swapaxes(2, 3),
+        jnp.concatenate([gate_second, up_second], axis=3),
+        jnp.concatenate([down_first[:, :pairs], down_first[:, pairs:]], axis=3),
+        down_second,
+    )
     vmem = pl.BlockSpec(memory_space=pltpu.VMEM)
     dma = pltpu.SemaphoreType.DMA
-    out, counts = pl.pallas_call(
-        functools.partial(expert_kernel, (groups, dp, top_k, cap)),
+    out, load = pl.pallas_call(
+        functools.partial(expert_kernel, (groups, dp, top_k, cap, rank_here, block_count)),
         out_shape=(
             jax.ShapeDtypeStruct((tok_rows, features), BF16),
-            jax.ShapeDtypeStruct((8, tok_rows), F32),
+            jax.ShapeDtypeStruct((1, per_dev), F32),
         ),
         in_specs=[vmem] * 8,
         out_specs=(vmem, vmem),
         scratch_shapes=[
-            pltpu.VMEM((groups, tok_rows, features), BF16),
-            pltpu.VMEM((groups, 2 * top_k, tok_rows), F32),
+            pltpu.VMEM((nz, tok_rows, features), BF16),
+            pltpu.VMEM((nz, top_k, tok_rows), jnp.int32),
+            pltpu.VMEM((nz, top_k, tok_rows), F32),
+            *[pltpu.VMEM(factor.shape, BF16) for factor in factors],
             pltpu.VMEM((per_dev, blocks, width, dp * chunk), BF16),
             pltpu.VMEM((per_dev, 2 * dp, chunk, 2 * hidden), BF16),
             pltpu.VMEM((per_dev, rank_here, block_count, hidden), BF16),
@@ -472,27 +495,25 @@
             pltpu.VMEM((2 * dp, chunk, 2 * hidden), F32),
             pltpu.VMEM((slots, features), BF16),
             pltpu.VMEM((2, dp, 2, slots, chunk), BF16),
-            pltpu.VMEM((groups, dp, 2, slots, chunk), BF16),
+            pltpu.VMEM((steps, dp, 2, slots, chunk), BF16),
             pltpu.VMEM((2, dp, slots, chunk), BF16),
-            pltpu.VMEM((groups, dp, slots, chunk), BF16),
-            pltpu.VMEM((groups, tok_rows, slots), BF16),
+            pltpu.VMEM((steps, dp, slots, chunk), BF16),
+            pltpu.VMEM((steps, tok_rows, slots), BF16),
             pltpu.VMEM((slots, features), BF16),
+            pltpu.VMEM((nz, tok_rows, features), F32),
             pltpu.VMEM((nz, tok_rows, features), BF16),
             pltpu.VMEM((nz, tok_rows, features), BF16),
-            pltpu.VMEM((nz, tok_rows, features), BF16),
-            pltpu.VMEM((nz, tok_rows, features), BF16),
-            pltpu.VMEM((nz, tok_rows, features), BF16),
-            dma((nz,)), dma((nz,)), dma((groups,)),
-            dma((nz,)), dma((nz,)), dma((groups,)),
-            dma((2, dp)), dma((groups, dp)), dma((2, dp)), dma((groups, dp)),
-            dma((2,)), dma((nz,)), dma((nz,)), dma((nz,)), dma((nz,)),
+            pltpu.VMEM((2, 8, tok_rows), F32),
+            pltpu.VMEM((8, tok_rows), F32),
+            dma((3, nz)), dma((3, nz)), dma((5,)), dma((5,)),
+            dma((2, dp)), dma((steps, dp)), dma((2, dp)), dma((steps, dp)),
+            dma((2,)), dma((2,)), dma((nz,)), dma((nz,)),
         ],
         compiler_params=pltpu.CompilerParams(
             collective_id=0, has_side_effects=True, vmem_limit_bytes=67043328
         ),
-    )(tokens, meta, *weights)
-    held = jnp.sum(counts, axis=1)[:per_dev]
-    return (out, held * experts / (tok_rows * groups * top_k))
+    )(tokens, routes.T, route_weight.T, *factors)
+    return (out, load.reshape(per_dev))
 
 
 def chosen_plan(tokens, routes, route_weight, *weights):

time: 137 us -> 130 us (0.949); the launches traced: 135 us -> 130 us
  local copies, waits for them, and re-layouts: 6.02 us -> 3.66 us
  other arithmetic: 3.34 us -> 1.95 us
    unnamed x5 -> x8, local copies, waits for them, and re-layouts: 6.02 us -> 2.52 us
    pallas_call x1, Pallas kernels: 125 us -> 124 us  [fused(): pl.pallas_call(functools.partial(expert_kernel, (groups, dp, top_k, cap,...]
where the time goes in v3:
time: 130 us
  Pallas kernels  124 us (95%)
  local copies, waits for them, and re-layouts  3.66 us (3%)
  other arithmetic  1.95 us (2%)
    pallas_call x1, Pallas kernels, fused(): pl.pallas_call(functools.partial(expert_kernel, (groups, dp, top_k, cap,...  124 us

profile of v3, /device:TPU:0, one launch (start us, length us, event | category | flops | bytes accessed | tf_op | source)
XLA Modules:
  0.0 129.9 jit_solution(17969350881516084892)
XLA Ops:
  0.6 0.0 copy-start.1
  0.6 1.1 fusion
  1.8 0.0 copy-start
  1.8 0.9 pad_maximum_fusion.1.df
  2.7 0.0 copy-done.1
  2.7 0.2 copy-done
  2.8 1.1 pad_maximum_fusion.gs
  3.9 123.6 %shard_map.104 = (bf16[128,1792]{1,0:T(8,128)(2,1)}, f32[1,4]{1,0:T(1,128)}) custom-call(bf16[128,1792]{1,0:T(8,128)(2,1)} %tok.1, s32[8,128]{1,0:T(8,128)} %bitcast.7, f32[8,128]{1,0:T(8,128)} %bitcast.8, bf16[4,16,32,112]{3,2,1,0:T(8,128)(2,1)} %bitcast.5, bf16[4,16,32,112]{3,2,1,0:T(8,128)(2,1)} %bitcast.6, bf16[4,8,64,128]{3,2,1,0:T(8,128)(2,1)} %pad_maximum_fusion.gs, ...), custom_call_target="tpu_custom_call" | custom-call | tf_op jit(solution)/shard_map/pallas_call | solution.py:478
  127.6 0.0 copy-start.2
  127.6 1.8 %copy.13 = bf16[128,1792]{1,0:T(8,128)(2,1)} copy(bf16[128,1792]{1,0:T(8,128)(2,1)} %get-tuple-element.10) | data formatting | bytes 917504
  129.4 0.0 copy-done.2
  129.4 0.5 copy.14
Async XLA Ops:
  0.6 2.0 %copy-start.1 = (bf16[4,8,64,64]{3,2,1,0:T(8,128)(2,1)S(1)}, bf16[4,8,64,64]{3,2,1,0:T(8,128)(2,1)}, u32[]{:S(2)}) copy-start(bf16[4,8,64,64]{3,2,1,0:T(8,128)(2,1)} %param.14) | copy-start | bytes 786436
  1.8 1.1 copy-start
  127.6 1.8 %copy-start.2 = (f32[1,4]{1,0:T(1,128)S(1)}, f32[1,4]{1,0:T(1,128)}, u32[]{:S(2)}) copy-start(f32[1,4]{1,0:T(1,128)} %get-tuple-element.5) | copy-start | bytes 52

commit v4 on v3

--- a/solution.py
+++ b/solution.py
@@ -202,17 +202,21 @@
 
     def spread_middle(second, third):
         wide[...] = jnp.zeros_like(wide)
+        lanes = sorted({(c * block_count) % 128 for c in range(rank_here)})
+        places = {
+            (side, lane): ones_at(
+                (2, block_count, 128), lambda s, r: jnp.where(s == side, r + lane, -1)
+            )
+            for side in range(2)
+            for lane in lanes
+        }
 
         @pl.loop(0, per_dev)
         def _(e):
             for side in range(2):
                 for c in range(rank_here):
                     lane = (c * block_count) % 128
-                    place = ones_at(
-                        (2, block_count, 128),
-                        lambda s, r: jnp.where(s == side, r + lane, -1),
-                    )
-                    value = dot(second[e, c], place)
+                    value = dot(second[e, c], places[side, lane])
                     row = side * (chunk // 2) + c * half
                     start = side * hidden + c * block_count - lane
                     wide[:, row : row + half, start : start + 128] = value.reshape(
@@ -233,6 +237,11 @@
 
     def spread_last(fourth):
         wide[...] = jnp.zeros_like(wide)
+        places = {}
+        for j in range(half):
+            lane = (j * width) % 128
+            span = -(-(lane + width) // 128) * 128
+            places[j] = ones_at((width, span), lambda r: r + lane)
 
         @pl.loop(0, per_dev)
         def _(e):
@@ -241,7 +250,7 @@
                 offset = (n % half) * width
                 lane = offset % 128
                 span = -(-(lane + width) // 128) * 128
-                value = dot(fourth[e, n], ones_at((width, span), lambda r: r + lane))
+                value = dot(fourth[e, n], places[n % half])
                 wide[
                     h * dp : (h + 1) * dp,
                     n * rank_here : (n + 1) * rank_here,

time: 130 us -> 130 us (level)
  no operation moved by 1% of the time
where the time goes in v4:
time: 130 us
  Pallas kernels  124 us (95%)
  local copies, waits for them, and re-layouts  3.66 us (3%)
  other arithmetic  1.95 us (2%)
    pallas_call x1, Pallas kernels, fused(): pl.pallas_call(functools.partial(expert_kernel, (groups, dp, top_k, cap,...  124 us

profile of v4, /device:TPU:0, one launch (start us, length us, event | category | flops | bytes accessed | tf_op | source)
XLA Modules:
  0.0 129.9 jit_solution(1543942399712360891)
XLA Ops:
  0.6 0.0 copy-start.1
  0.6 1.1 fusion
  1.8 0.0 copy-start
  1.8 0.9 pad_maximum_fusion.1.df
  2.7 0.0 copy-done.1
  2.7 0.2 copy-done
  2.8 1.1 pad_maximum_fusion.gs
  3.9 123.7 %shard_map.104 = (bf16[128,1792]{1,0:T(8,128)(2,1)}, f32[1,4]{1,0:T(1,128)}) custom-call(bf16[128,1792]{1,0:T(8,128)(2,1)} %tok.1, s32[8,128]{1,0:T(8,128)} %bitcast.7, f32[8,128]{1,0:T(8,128)} %bitcast.8, bf16[4,16,32,112]{3,2,1,0:T(8,128)(2,1)} %bitcast.5, bf16[4,16,32,112]{3,2,1,0:T(8,128)(2,1)} %bitcast.6, bf16[4,8,64,128]{3,2,1,0:T(8,128)(2,1)} %pad_maximum_fusion.gs, ...), custom_call_target="tpu_custom_call" | custom-call | tf_op jit(solution)/shard_map/pallas_call | solution.py:487
  127.6 0.0 copy-start.2
  127.6 1.8 %copy.13 = bf16[128,1792]{1,0:T(8,128)(2,1)} copy(bf16[128,1792]{1,0:T(8,128)(2,1)} %get-tuple-element.10) | data formatting | bytes 917504
  129.4 0.0 copy-done.2
  129.4 0.5 copy.14
Async XLA Ops:
  0.6 2.0 %copy-start.1 = (bf16[4,8,64,64]{3,2,1,0:T(8,128)(2,1)S(1)}, bf16[4,8,64,64]{3,2,1,0:T(8,128)(2,1)}, u32[]{:S(2)}) copy-start(bf16[4,8,64,64]{3,2,1,0:T(8,128)(2,1)} %param.14) | copy-start | bytes 786436
  1.8 1.1 copy-start
  127.6 1.8 %copy-start.2 = (f32[1,4]{1,0:T(1,128)S(1)}, f32[1,4]{1,0:T(1,128)}, u32[]{:S(2)}) copy-start(f32[1,4]{1,0:T(1,128)} %get-tuple-element.5) | copy-start | bytes 52
